TPU v7x, 512 devices: a whole 4x8x8 slice. The times are simulated.
512 devices in a mesh: row: 16 (over z, core), col: 32 (over y, x).
Axes of the slice: x: 4, y: 8, z: 8, core: 2. Of those that a mesh axis runs over, the one named last changes fastest.
Arguments:
- initial_voltage: float32 [16, 64, 128, 128], P('row', 'col'), may hold values from -6 to 6
- inject: float32 [16, 64, 128, 128], P('row', 'col'), may hold values from -6 to 6
- conduct: float32 [16, 64, 128, 128], P('row', 'col'), as said below
- capacitance: float32 [16, 64, 128], P('row', 'col'), may hold values from 1 to 4
- track_gain: float32 [16, 64, 2, 32], P('row', 'col'), may hold values from 0.3 to 3
- driver_tile: int32 [16, 32, 64], P('row', 'col'), may hold values from 0 to 1
- sink_net: int32 [16, 32, 32, 8], P('row', 'col'), may hold values from 0 to 63
- sink_count: int32 [16, 32, 32], P('row', 'col'), may hold values from 0 to 8, as said below
- sink_tile: int32 [16, 32, 32, 8], P('row', 'col'), may hold values from 0 to 1
- sink_node: int32 [16, 32, 32, 8], P('row', 'col'), may hold values from 0 to 127
- sink_gain: float32 [16, 32, 32, 8], P('row', 'col'), may hold values from 0.5 to 2
Outputs:
- voltage: float32 [16, 64, 128, 128], P('row', 'col')
Inputs may be any that keep to these rules, and one draw needn't show every extreme that they name: Slots k >= sink_count[d, s] are ignored; some receiving device takes all 8 slots from some source device in every draw. `conduct`: each tile's block is symmetric with non-positive entries off the diagonal and rows summing to zero.
All inputs are finite; a program needn't handle non-finite values.
Results may differ from a plain program's by a relative error of at most 0.0001.
Values sent between devices are 32-bit elements; how exact they have to be, the bound alone decides.
A program may use at most 64 MiB of HBM per device.

v0:
```python
import jax
import jax.numpy as jnp
from jax import lax
from jax.sharding import PartitionSpec as P

ITERS = 3
PRECISE = lax.Precision.HIGHEST


def padded_2(block, sides, width):
    for axis, dim in sides:
        count = lax.axis_size(axis)
        forward = [(i, i + 1) for i in range(count - 1)]
        backward = [(target, source) for source, target in forward]
        low = lax.ppermute(
            lax.slice_in_dim(block, block.shape[dim] - width, None, axis=dim), axis, forward
        )
        high = lax.ppermute(lax.slice_in_dim(block, 0, width, axis=dim), axis, backward)
        block = jnp.concatenate([low, block, high], axis=dim)
    return block


def shifted(block, axis, distance):
    devices = range(lax.axis_size(axis))
    route = [(i - distance, i) for i in devices if i - distance in devices]
    return lax.ppermute(block, axis, route)


def tile_inverse(conduct, capacitance):
    node_count = conduct.shape[-1]
    identity = jnp.eye(node_count, dtype=jnp.float32)
    whole_block = conduct + capacitance[..., None] * identity
    flat_blocks = whole_block.reshape((-1, node_count, node_count))
    factors = jnp.linalg.cholesky(flat_blocks)
    inverse = jax.vmap(lambda factor: jax.scipy.linalg.cho_solve((factor, True), identity))(factors)
    return inverse.reshape(whole_block.shape)


def apply_grid(voltage, conduct, capacitance, track_pad):
    edge_count = track_pad.shape[-1]
    inner_part = (
        jnp.einsum("rcij,rcjp->rcip", conduct, voltage, precision=PRECISE)
        + capacitance[..., None] * voltage
    )
    rim_cells = voltage[:, :, :edge_count, :]
    padded = padded_2(rim_cells, (("row", 0), ("col", 1)), 1)
    east_gain = track_pad[1:-1, 1:-1, 0][..., None]
    west_gain = track_pad[1:-1, :-2, 0][..., None]
    south_gain = track_pad[1:-1, 1:-1, 1][..., None]
    north_gain = track_pad[:-2, 1:-1, 1][..., None]
    track_flow = east_gain * (rim_cells - padded[1:-1, 2:]) + west_gain * (
        rim_cells - padded[1:-1, :-2]
    )
    track_flow = (
        track_flow
        + south_gain * (rim_cells - padded[2:, 1:-1])
        + north_gain * (rim_cells - padded[:-2, 1:-1])
    )
    return jnp.concatenate(
        [inner_part[:, :, :edge_count] + track_flow, inner_part[:, :, edge_count:]], axis=2
    )


def precondition(inverse, residual):
    return jnp.einsum("rcij,rcjp->rcip", inverse, residual, precision=PRECISE)


def inner_sum(left_vec, right_vec):
    return jnp.sum(left_vec * right_vec, axis=(0, 1, 2))


def residual_product(residual, precond):
    return lax.psum(inner_sum(residual, precond), ("row", "col"))


def solve_separate(right_side, initial, conduct, capacitance, track_pad, inverse):
    solution = initial
    residual = right_side - apply_grid(initial, conduct, capacitance, track_pad)
    precond = precondition(inverse, residual)
    direction = precond
    rz_now = residual_product(residual, precond)
    for sweep_idx in range(ITERS):
        applied = apply_grid(direction, conduct, capacitance, track_pad)
        curvature = lax.psum(inner_sum(direction, applied), ("row", "col"))
        step_size = rz_now / curvature
        solution = solution + step_size * direction
        residual = residual - step_size * applied
        precond = precondition(inverse, residual)
        rz_fresh = residual_product(residual, precond)
        direction = precond + rz_fresh / rz_now * direction
        rz_now = rz_fresh
    return solution


def driver_voltage(voltage, driver_tile):
    node_count = voltage.shape[2]
    flat_field = voltage.reshape((-1, voltage.shape[3]))
    net_count = driver_tile.shape[-1]
    row_index = (
        driver_tile.reshape(-1) * node_count + jnp.arange(net_count, dtype=jnp.int32) % node_count
    )
    return jnp.take(flat_field, row_index, axis=0)


def sink_current(values, sink_tile, sink_node, sink_gain, sink_count, node_count, tile_count):
    source_count, slot_count, pattern_count = values.shape
    live_slot = jnp.arange(slot_count, dtype=jnp.int32)[None, :] < sink_count.reshape(
        (source_count, 1)
    )
    weight = jnp.where(live_slot, sink_gain.reshape((source_count, slot_count)), jnp.float32(0.0))
    row_index = (sink_tile * node_count + sink_node).reshape(-1)
    scaled = (values * weight[..., None]).reshape((-1, pattern_count))
    injected = jnp.zeros((tile_count * node_count, pattern_count), jnp.float32)
    return injected.at[row_index].add(scaled)


def lower_rims(track_gain):
    west_piece = shifted(track_gain[:, -1:, 0, :], "col", 1)
    north_piece = shifted(track_gain[-1:, :, 1, :], "row", 1)
    track_pad = jnp.pad(track_gain, ((1, 1), (1, 1), (0, 0), (0, 0)))
    track_pad = track_pad.at[1:-1, 0, 0].set(west_piece[:, 0])
    return track_pad.at[0, 1:-1, 1].set(north_piece[0])


def local(
    initial_voltage,
    inject,
    conduct,
    capacitance,
    track_gain,
    driver_tile,
    sink_net,
    sink_count,
    sink_tile,
    sink_node,
    sink_gain,
):
    inverse = tile_inverse(conduct, capacitance)
    track_pad = lower_rims(track_gain)
    col_count = lax.axis_size("col")
    net_count = driver_tile.shape[-1]
    pattern_count = initial_voltage.shape[3]
    node_count = initial_voltage.shape[2]
    tile_count = initial_voltage.shape[0] * initial_voltage.shape[1]
    wanted = sink_net.reshape((sink_net.shape[2], sink_net.shape[3]))
    voltage = initial_voltage
    drivers = driver_voltage(voltage, driver_tile)
    gathered = lax.all_gather(drivers, "col", axis=0, tiled=True)
    offsets = jnp.arange(col_count, dtype=jnp.int32)[:, None] * net_count
    values = jnp.take(gathered, (wanted + offsets).reshape(-1), axis=0).reshape(
        wanted.shape + (pattern_count,)
    )
    injected = sink_current(
        values, sink_tile, sink_node, sink_gain, sink_count, node_count, tile_count
    )
    right_side = capacitance[..., None] * voltage + inject + injected.reshape(voltage.shape)
    voltage = solve_separate(right_side, voltage, conduct, capacitance, track_pad, inverse)
    return voltage


def solution(mesh):
    placed = (
        P("row", "col", None, None),
        P("row", "col", None, None),
        P("row", "col", None, None),
        P("row", "col", None),
        P("row", "col", None, None),
        P("row", "col", None),
        P("row", "col", None, None),
        P("row", "col", None),
        P("row", "col", None, None),
        P("row", "col", None, None),
        P("row", "col", None, None),
    )
    return jax.shard_map(
        local, mesh=mesh, in_specs=placed, out_specs=P("row", "col", None, None), check_vma=False
    )
```

profile of v0, /device:TPU:1, one launch (start us, length us, event | category | flops | bytes accessed | tf_op | source)
XLA Modules:
  0.0 707.5 jit_solution(17942465035946714458)
XLA Ops:
  6.5 1.1 copy.150
  7.6 8.8 %collective-permute-start.2 = (f32[1,2,32,128]{2,3,1,0:T(8,128)S(1)}, f32[1,2,32,128]{2,3,1,0:T(8,128)S(1)}, u32[]{:S(2)}, u32[]{:S(2)}) collective-permute-start(f32[1,2,32,128]{2,3,1,0:T(8,128)S(1)} %bitcast.150), channel_id=1, source_target_pairs={{32,0},{64,32},{96,64},{128,96},{160,128},{192,160},{224,192},{256... | collective-permute-start | bytes 98312 | tf_op jit(solution)/shard_map/ppermute | solution.py:18
  16.4 1.9 collective-permute-start.1
  18.4 1.3 collective-permute-start
  19.7 1.9 collective-permute-start.5
  29.1 1.3 collective-permute-start.3
  30.4 4.0 collective-permute-start.4
  34.5 1.1 collective-permute-done.4
  35.9 66.4 %all-gather.2.cloned.1.call-done = f32[2048,128]{1,0:T(8,128)} async-done(((f32[64,128]{1,0:T(8,128)}), f32[2048,128]{1,0:T(8,128)}) %all-gather.2.cloned.1.call-update) | async-done | bytes 1048592 | tf_op jit(solution)/shard_map/all_gather | solution.py:148
  102.3 3.4 scatter_custom_fusion
  106.0 23.5 %custom-call.11 = f32[2,128,128]{2,1,0:T(8,128)S(1)} custom-call(f32[2,128,128]{2,1,0:T(8,128)S(1)} %fusion.13), custom_call_target="Cholesky" | custom-call | tf_op jit(solution)/shard_map/jit(cholesky)/cholesky | solution.py:34
  129.8 19.7 %custom-call.12 = f32[2,1,128,128]{2,3,1,0:T(8,128)S(1)} custom-call(f32[2,1,128,128]{3,2,1,0:T(8,128)S(1)} %select_bitcast_fusion), custom_call_target="InvertDiagBlocksLowerTriangular" | custom-call | tf_op jit(solution)/shard_map/vmap(jit(_cho_solve))/triangular_solve | solution.py:35
  151.0 6.9 collective-permute-start.7
  157.9 3.2 collective-permute-start.6
  161.9 1.2 collective-permute-done.6
  163.1 1.3 collective-permute-start.8
  164.4 4.0 collective-permute-start.9
  170.1 103.8 %all-reduce.1 = (f32[128]{0:T(128)S(1)}, f32[128]{0:T(128)S(1)}) all-reduce(f32[128]{0:T(128)S(1)} %multiply_reduce_fusion, f32[128]{0:T(128)S(1)} %fusion.8), channel_id=1, replica_groups=mesh['row'=16,'col'=32] {'row','col'}, use_global_device_ids=true, to_apply=%region_4.5 | all-reduce | flops 256 | bytes 2048 | tf_op jit(solution)/shard_map/psum | solution.py:73
  274.5 95.4 %psum.44 = f32[128]{0:T(128)S(1)} all-reduce(f32[128]{0:T(128)S(1)} %get-tuple-element.56), channel_id=1, replica_groups=mesh['row'=16,'col'=32] {'row','col'}, use_global_device_ids=true, to_apply=%region_8.9 | all-reduce | flops 128 | bytes 1024 | tf_op jit(solution)/shard_map/psum | solution.py:73
  370.0 2.6 collective-permute-start.11
  372.6 3.3 collective-permute-start.10
  376.7 1.2 collective-permute-done.10
  377.9 1.3 collective-permute-start.12
  379.2 4.0 collective-permute-start.13
  384.8 102.0 %psum.45 = f32[128]{0:T(128)S(1)} all-reduce(f32[128]{0:T(128)S(1)} %fusion.10), channel_id=1, replica_groups=mesh['row'=16,'col'=32] {'row','col'}, use_global_device_ids=true, to_apply=%region_10.11 | all-reduce | flops 128 | bytes 1024 | tf_op jit(solution)/shard_map/psum | solution.py:84
  487.4 95.3 %psum.46 = f32[128]{0:T(128)S(1)} all-reduce(f32[128]{0:T(128)S(1)} %get-tuple-element.58), channel_id=1, replica_groups=mesh['row'=16,'col'=32] {'row','col'}, use_global_device_ids=true, to_apply=%region_12.13 | all-reduce | flops 128 | bytes 1024 | tf_op jit(solution)/shard_map/psum | solution.py:73
  582.7 2.6 collective-permute-start.15
  585.3 3.5 collective-permute-start.14
  589.6 1.2 collective-permute-done.14
  590.8 1.3 collective-permute-start.16
  592.1 4.0 collective-permute-start.17
  597.8 102.0 %psum.47 = f32[128]{0:T(128)S(1)} all-reduce(f32[128]{0:T(128)S(1)} %fusion.12), channel_id=1, replica_groups=mesh['row'=16,'col'=32] {'row','col'}, use_global_device_ids=true, to_apply=%region_14.15 | all-reduce | flops 128 | bytes 1024 | tf_op jit(solution)/shard_map/psum | solution.py:84
  (144 shorter events, 19.2 us)
Async XLA Ops:
  6.5 15.1 %copy-start.1 = (f32[1,2,128,128]{3,2,1,0:T(8,128)S(1)}, f32[1,2,128,128]{3,2,1,0:T(8,128)}, u32[]{:S(2)}) copy-start(f32[1,2,128,128]{3,2,1,0:T(8,128)} %param.15) | copy-start | bytes 393220
  6.5 11.8 %copy-start.4 = (f32[1,2,2,32]{3,2,1,0:T(2,128)S(1)}, f32[1,2,2,32]{3,2,1,0:T(2,128)}, u32[]{:S(2)}) copy-start(f32[1,2,2,32]{3,2,1,0:T(2,128)} %param.19) | copy-start | bytes 1540
  6.5 95.8 %all-gather.2.cloned.1.call-start = ((), (), s32[]{:S(2)}) async-start(), calls=%async_computation | async-start | bytes 1081344 | tf_op jit(solution)/shard_map/all_gather | solution.py:148
  7.6 21.3 %collective-permute-start.2 = (f32[1,2,32,128]{2,3,1,0:T(8,128)S(1)}, f32[1,2,32,128]{2,3,1,0:T(8,128)S(1)}, u32[]{:S(2)}, u32[]{:S(2)}) collective-permute-start(f32[1,2,32,128]{2,3,1,0:T(8,128)S(1)} %bitcast.150), channel_id=1, source_target_pairs={{32,0},{64,32},{96,64},{128,96},{160,128},{192,160},{224,192},{256... | collective-permute-start | bytes 98312 | tf_op jit(solution)/shard_map/ppermute | solution.py:18
  16.4 12.6 %collective-permute-start.1 = (f32[1,2,32,128]{2,3,1,0:T(8,128)S(1)}, f32[1,2,32,128]{2,3,1,0:T(8,128)S(1)}, u32[]{:S(2)}, u32[]{:S(2)}) collective-permute-start(f32[1,2,32,128]{2,3,1,0:T(8,128)S(1)} %bitcast.151), channel_id=1, source_target_pairs={{0,32},{32,64},{64,96},{96,128},{128,160},{160,192},{192,224},{224... | collective-permute-start | bytes 98312 | tf_op jit(solution)/shard_map/ppermute | solution.py:15
  18.4 10.5 %collective-permute-start = (f32[1,1,32]{2,1,0:T(1,128)S(1)}, f32[1,1,32]{2,1,0:T(1,128)S(1)}, u32[]{:S(2)}, u32[]{:S(2)}) collective-permute-start(f32[1,1,32]{2,1,0:T(1,128)S(1)} %slice_bitcast_fusion.1), channel_id=1, source_target_pairs={{0,1},{1,2},{2,3},{3,4},{4,5},{5,6},{6,7},{7,8},{8,9},{9,10},{10,1... | collective-permute-start | bytes 392 | tf_op jit(solution)/shard_map/ppermute | solution.py:26
  19.7 1.9 copy-start.10
  19.7 16.1 %collective-permute-start.5 = (f32[1,2,32]{2,1,0:T(2,128)S(1)}, f32[1,2,32]{2,1,0:T(2,128)S(1)}, u32[]{:S(2)}, u32[]{:S(2)}) collective-permute-start(f32[1,2,32]{2,1,0:T(2,128)S(1)} %bitcast.184), channel_id=1, source_target_pairs={{0,32},{32,64},{64,96},{96,128},{128,160},{160,192},{192,224},{224... | collective-permute-start | bytes 776 | tf_op jit(solution)/shard_map/ppermute | solution.py:26
  23.2 0.7 copy-start.5
  23.8 2.7 copy-start
  24.1 0.7 copy-start.9
  24.8 0.7 copy-start.6
  24.8 0.7 copy-start.7
  25.6 0.7 copy-start.8
  26.5 0.7 copy-start.3
  27.9 0.9 copy-start.2
  29.1 5.3 collective-permute-start.3
  30.4 5.2 collective-permute-start.4
  151.0 10.8 %collective-permute-start.7 = (f32[1,2,32,128]{2,3,1,0:T(8,128)S(1)}, f32[1,2,32,128]{2,3,1,0:T(8,128)S(1)}, u32[]{:S(2)}, u32[]{:S(2)}) collective-permute-start(f32[1,2,32,128]{2,3,1,0:T(8,128)S(1)} %bitcast.142), channel_id=1, source_target_pairs={{32,0},{64,32},{96,64},{128,96},{160,128},{192,160},{224,192},{256... | collective-permute-start | bytes 98312 | tf_op jit(solution)/shard_map/ppermute | solution.py:18
  157.9 5.1 collective-permute-start.6
  163.1 5.4 collective-permute-start.8
  164.4 5.2 collective-permute-start.9
  370.0 6.6 collective-permute-start.11
  372.6 5.2 collective-permute-start.10
  377.9 5.4 collective-permute-start.12
  379.2 5.2 collective-permute-start.13
  582.7 6.8 collective-permute-start.15
  585.3 5.4 collective-permute-start.14
  590.8 5.4 collective-permute-start.16
  592.1 5.2 collective-permute-start.17
Sparse Core Ops, SparseCore 0:
  23.1 79.1 all-gather.1
where the time goes:
time: 709 us; the launch traced here: 707 us
  blocking collectives  498 us (70%)
  waiting for transfers between devices  75.2 us (11%)
  starting transfers between devices  57 us (8%)
  other arithmetic  49.2 us (7%)
  between operations  14.1 us (2%)
  local copies, waits for them, and re-layouts  9.8 us (1%)
    psum x3, blocking collectives, residual_product(): return lax.psum(inner_sum(residual, precond), ('row', 'col'))  295 us
    psum x2, blocking collectives, solve_separate(): curvature = lax.psum(inner_sum(direction, applied), ('row', 'col'))  204 us
    all_gather x1, waiting for transfers between devices, local(): gathered = lax.all_gather(drivers, 'col', axis=0, tiled=True)  66.4 us
    ppermute x8, starting transfers between devices, padded_2(): lax.ppermute(lax.slice_in_dim(block, block.shape[dim] - width, None, axis...  27.8 us
    ppermute x8, starting transfers between devices, padded_2(): lax.ppermute(lax.slice_in_dim(block, 0, width, axis=dim), axis, backward)  26 us
    another operation x4, other arithmetic, tile_inverse(): factors = jnp.linalg.cholesky(flat_blocks)  23.6 us
    another operation x3, other arithmetic, tile_inverse(): jax.scipy.linalg.cho_solve((factor, True), identity)  19.8 us
  transfers between devices with their start and end apart: 19, of which 11 were waited for; matrix products, arithmetic and copies ran while one was open for 1% of the time, Pallas kernels for 0%

commit v1 on v0

--- a/solution.py
+++ b/solution.py
@@ -70,7 +70,7 @@
 
 
 def residual_product(residual, precond):
-    return lax.psum(inner_sum(residual, precond), ("row", "col"))
+    return jnp.sum(lax.all_gather(inner_sum(residual, precond), ("row", "col")), axis=0)
 
 
 def solve_separate(right_side, initial, conduct, capacitance, track_pad, inverse):

time: 709 us -> 801 us (1.13)
  blocking collectives: 498 us -> 591 us
    psum x3 -> x0, blocking collectives: 295 us -> none  [residual_product(): return lax.psum(inner_sum(residual, precond), ('row', 'col'))]
    all_gather x0 -> x3, blocking collectives: none -> 291 us  [residual_product(): lax.all_gather(inner_sum(residual, precond), ('row', 'col'))]
    psum x2 -> x3, blocking collectives: 204 us -> 300 us  [solve_separate(): curvature = lax.psum(inner_sum(direction, applied), ('row', 'col'))]
  transfers between devices with their start and end apart: 19 -> 19, of which waited for: 11 -> 10; matrix products, arithmetic and copies ran while one was open for 1% -> 1% of each run, Pallas kernels for 0% -> 0%
where the time goes in v1:
time: 801 us; the launch traced here: 800 us
  blocking collectives  591 us (74%)
  waiting for transfers between devices  74.2 us (9%)
  starting transfers between devices  56.9 us (7%)
  other arithmetic  50.9 us (6%)
  between operations  14.1 us (2%)
  local copies, waits for them, and re-layouts  9.81 us (1%)
    psum x3, blocking collectives, solve_separate(): curvature = lax.psum(inner_sum(direction, applied), ('row', 'col'))  300 us
    all_gather x3, blocking collectives, residual_product(): lax.all_gather(inner_sum(residual, precond), ('row', 'col'))  291 us
    all_gather x1, waiting for transfers between devices, local(): gathered = lax.all_gather(drivers, 'col', axis=0, tiled=True)  66.4 us
    ppermute x8, starting transfers between devices, padded_2(): lax.ppermute(lax.slice_in_dim(block, 0, width, axis=dim), axis, backward)  28.1 us
    ppermute x8, starting transfers between devices, padded_2(): lax.ppermute(lax.slice_in_dim(block, block.shape[dim] - width, None, axis...  25.6 us
    another operation x4, other arithmetic, tile_inverse(): factors = jnp.linalg.cholesky(flat_blocks)  23.6 us
    another operation x3, other arithmetic, tile_inverse(): jax.scipy.linalg.cho_solve((factor, True), identity)  19.8 us
  transfers between devices with their start and end apart: 19, of which 10 were waited for; matrix products, arithmetic and copies ran while one was open for 1% of the time, Pallas kernels for 0%

profile of v1, /device:TPU:1, one launch (start us, length us, event | category | flops | bytes accessed | tf_op | source)
XLA Modules:
  0.0 800.2 jit_solution(13012872768503071728)
XLA Ops:
  7.6 8.8 %collective-permute-start.2 = (f32[1,2,32,128]{2,3,1,0:T(8,128)S(1)}, f32[1,2,32,128]{2,3,1,0:T(8,128)S(1)}, u32[]{:S(2)}, u32[]{:S(2)}) collective-permute-start(f32[1,2,32,128]{2,3,1,0:T(8,128)S(1)} %bitcast.153), channel_id=1, source_target_pairs={{32,0},{64,32},{96,64},{128,96},{160,128},{192,160},{224,192},{256... | collective-permute-start | bytes 98312 | tf_op jit(solution)/shard_map/ppermute | solution.py:18
  16.4 1.9 collective-permute-start.1
  18.4 1.3 collective-permute-start
  19.7 1.9 collective-permute-start.5
  29.1 1.3 collective-permute-start.3
  30.4 4.0 collective-permute-start.4
  34.5 1.1 collective-permute-done.4
  35.9 66.4 %all-gather.8.cloned.1.call-done = f32[2048,128]{1,0:T(8,128)} async-done(((f32[64,128]{1,0:T(8,128)}), f32[2048,128]{1,0:T(8,128)}) %all-gather.8.cloned.1.call-update) | async-done | bytes 1048592 | tf_op jit(solution)/shard_map/all_gather | solution.py:148
  102.3 3.4 scatter_custom_fusion
  106.0 23.5 %custom-call.11 = f32[2,128,128]{2,1,0:T(8,128)S(1)} custom-call(f32[2,128,128]{2,1,0:T(8,128)S(1)} %fusion.13), custom_call_target="Cholesky" | custom-call | tf_op jit(solution)/shard_map/jit(cholesky)/cholesky | solution.py:34
  129.7 19.7 %custom-call.12 = f32[2,1,128,128]{2,3,1,0:T(8,128)S(1)} custom-call(f32[2,1,128,128]{3,2,1,0:T(8,128)S(1)} %select_bitcast_fusion), custom_call_target="InvertDiagBlocksLowerTriangular" | custom-call | tf_op jit(solution)/shard_map/vmap(jit(_cho_solve))/triangular_solve | solution.py:35
  151.0 6.9 collective-permute-start.7
  157.9 3.2 collective-permute-start.6
  161.9 1.2 collective-permute-done.6
  163.1 1.3 collective-permute-start.8
  164.4 4.0 collective-permute-start.9
  168.4 99.4 %all-gather.3 = f32[512,1,128]{2,1,0:T(1,128)S(1)} all-gather(f32[1,1,128]{2,1,0:T(1,128)S(1)} %bitcast.187), channel_id=2, replica_groups=mesh['row'=16,'col'=32] {'row','col'}, dimensions={0}, use_global_device_ids=true | all-gather | bytes 262656 | tf_op jit(solution)/shard_map/all_gather | solution.py:73
  268.8 97.6 %psum.21 = f32[128]{0:T(128)S(1)} all-reduce(f32[128]{0:T(128)S(1)} %fusion.8), channel_id=1, replica_groups=mesh['row'=16,'col'=32] {'row','col'}, use_global_device_ids=true, to_apply=%region_6.7 | all-reduce | flops 128 | bytes 1024 | tf_op jit(solution)/shard_map/psum | solution.py:84
  367.1 95.5 %all-gather.4 = f32[512,1,128]{2,1,0:T(1,128)S(1)} all-gather(f32[1,1,128]{2,1,0:T(1,128)S(1)} %bitcast.189), channel_id=3, replica_groups=mesh['row'=16,'col'=32] {'row','col'}, dimensions={0}, use_global_device_ids=true | all-gather | bytes 262656 | tf_op jit(solution)/shard_map/all_gather | solution.py:73
  463.3 3.0 collective-permute-start.11
  466.2 2.6 collective-permute-start.10
  469.6 1.2 collective-permute-done.10
  470.9 1.3 collective-permute-start.12
  472.2 4.0 collective-permute-start.13
  477.8 100.5 %psum.22 = f32[128]{0:T(128)S(1)} all-reduce(f32[128]{0:T(128)S(1)} %fusion.10), channel_id=1, replica_groups=mesh['row'=16,'col'=32] {'row','col'}, use_global_device_ids=true, to_apply=%region_10.11 | all-reduce | flops 128 | bytes 1024 | tf_op jit(solution)/shard_map/psum | solution.py:84
  578.8 96.1 %all-gather.5 = f32[512,1,128]{2,1,0:T(1,128)S(1)} all-gather(f32[1,1,128]{2,1,0:T(1,128)S(1)} %bitcast.188), channel_id=4, replica_groups=mesh['row'=16,'col'=32] {'row','col'}, dimensions={0}, use_global_device_ids=true | all-gather | bytes 262656 | tf_op jit(solution)/shard_map/all_gather | solution.py:73
  675.6 4.3 collective-permute-start.15
  679.9 1.9 collective-permute-start.14
  682.4 1.4 collective-permute-done.14
  683.9 1.3 collective-permute-start.16
  685.2 4.0 collective-permute-start.17
  690.9 101.6 %psum.23 = f32[128]{0:T(128)S(1)} all-reduce(f32[128]{0:T(128)S(1)} %fusion.12), channel_id=1, replica_groups=mesh['row'=16,'col'=32] {'row','col'}, use_global_device_ids=true, to_apply=%region_14.15 | all-reduce | flops 128 | bytes 1024 | tf_op jit(solution)/shard_map/psum | solution.py:84
  (148 shorter events, 20.7 us)
Async XLA Ops:
  6.5 15.1 %copy-start.1 = (f32[1,2,128,128]{3,2,1,0:T(8,128)S(1)}, f32[1,2,128,128]{3,2,1,0:T(8,128)}, u32[]{:S(2)}) copy-start(f32[1,2,128,128]{3,2,1,0:T(8,128)} %param.15) | copy-start | bytes 393220
  6.5 11.8 %copy-start.4 = (f32[1,2,2,32]{3,2,1,0:T(2,128)S(1)}, f32[1,2,2,32]{3,2,1,0:T(2,128)}, u32[]{:S(2)}) copy-start(f32[1,2,2,32]{3,2,1,0:T(2,128)} %param.19) | copy-start | bytes 1540
  6.5 95.8 %all-gather.8.cloned.1.call-start = ((), (), s32[]{:S(2)}) async-start(), calls=%async_computation | async-start | bytes 1081344 | tf_op jit(solution)/shard_map/all_gather | solution.py:148
  7.6 21.3 %collective-permute-start.2 = (f32[1,2,32,128]{2,3,1,0:T(8,128)S(1)}, f32[1,2,32,128]{2,3,1,0:T(8,128)S(1)}, u32[]{:S(2)}, u32[]{:S(2)}) collective-permute-start(f32[1,2,32,128]{2,3,1,0:T(8,128)S(1)} %bitcast.153), channel_id=1, source_target_pairs={{32,0},{64,32},{96,64},{128,96},{160,128},{192,160},{224,192},{256... | collective-permute-start | bytes 98312 | tf_op jit(solution)/shard_map/ppermute | solution.py:18
  16.4 12.6 %collective-permute-start.1 = (f32[1,2,32,128]{2,3,1,0:T(8,128)S(1)}, f32[1,2,32,128]{2,3,1,0:T(8,128)S(1)}, u32[]{:S(2)}, u32[]{:S(2)}) collective-permute-start(f32[1,2,32,128]{2,3,1,0:T(8,128)S(1)} %bitcast.154), channel_id=1, source_target_pairs={{0,32},{32,64},{64,96},{96,128},{128,160},{160,192},{192,224},{224... | collective-permute-start | bytes 98312 | tf_op jit(solution)/shard_map/ppermute | solution.py:15
  18.4 10.5 %collective-permute-start = (f32[1,1,32]{2,1,0:T(1,128)S(1)}, f32[1,1,32]{2,1,0:T(1,128)S(1)}, u32[]{:S(2)}, u32[]{:S(2)}) collective-permute-start(f32[1,1,32]{2,1,0:T(1,128)S(1)} %slice_bitcast_fusion.1), channel_id=1, source_target_pairs={{0,1},{1,2},{2,3},{3,4},{4,5},{5,6},{6,7},{7,8},{8,9},{9,10},{10,1... | collective-permute-start | bytes 392 | tf_op jit(solution)/shard_map/ppermute | solution.py:26
  19.7 1.9 copy-start.10
  19.7 16.1 %collective-permute-start.5 = (f32[1,2,32]{2,1,0:T(2,128)S(1)}, f32[1,2,32]{2,1,0:T(2,128)S(1)}, u32[]{:S(2)}, u32[]{:S(2)}) collective-permute-start(f32[1,2,32]{2,1,0:T(2,128)S(1)} %bitcast.190), channel_id=1, source_target_pairs={{0,32},{32,64},{64,96},{96,128},{128,160},{160,192},{192,224},{224... | collective-permute-start | bytes 776 | tf_op jit(solution)/shard_map/ppermute | solution.py:26
  23.2 0.7 copy-start.5
  23.8 2.7 copy-start
  24.1 0.7 copy-start.9
  24.8 0.7 copy-start.6
  24.8 0.7 copy-start.7
  25.6 0.7 copy-start.8
  26.5 0.7 copy-start.3
  27.9 0.9 copy-start.2
  29.1 5.3 collective-permute-start.3
  30.4 5.2 collective-permute-start.4
  151.0 10.8 %collective-permute-start.7 = (f32[1,2,32,128]{2,3,1,0:T(8,128)S(1)}, f32[1,2,32,128]{2,3,1,0:T(8,128)S(1)}, u32[]{:S(2)}, u32[]{:S(2)}) collective-permute-start(f32[1,2,32,128]{2,3,1,0:T(8,128)S(1)} %bitcast.145), channel_id=1, source_target_pairs={{32,0},{64,32},{96,64},{128,96},{160,128},{192,160},{224,192},{256... | collective-permute-start | bytes 98312 | tf_op jit(solution)/shard_map/ppermute | solution.py:18
  157.9 5.1 collective-permute-start.6
  163.1 105.2 %collective-permute-start.8 = (f32[3,1,32,128]{3,2,1,0:T(8,128)S(1)}, f32[3,1,32,128]{3,2,1,0:T(8,128)S(1)}, u32[]{:S(2)}, u32[]{:S(2)}) collective-permute-start(f32[3,1,32,128]{3,2,1,0:T(8,128)S(1)} %get-tuple-element.43), channel_id=1, source_target_pairs={{1,0},{2,1},{3,2},{4,3},{5,4},{6,5},{7,6},{8,7},{9,8},{10,9},{11,1... | collective-permute-start | bytes 147464 | tf_op jit(solution)/shard_map/ppermute | solution.py:18
  164.4 103.9 %collective-permute-start.9 = (f32[3,1,32,128]{3,2,1,0:T(8,128)S(1)}, f32[3,1,32,128]{3,2,1,0:T(8,128)S(1)}, u32[]{:S(2)}, u32[]{:S(2)}) collective-permute-start(f32[3,1,32,128]{3,2,1,0:T(8,128)S(1)} %get-tuple-element.44), channel_id=1, source_target_pairs={{0,1},{1,2},{2,3},{3,4},{4,5},{5,6},{6,7},{7,8},{8,9},{9,10},{10,1... | collective-permute-start | bytes 147464 | tf_op jit(solution)/shard_map/ppermute | solution.py:15
  463.3 6.3 collective-permute-start.11
  466.2 4.5 collective-permute-start.10
  470.9 5.4 collective-permute-start.12
  472.2 5.2 collective-permute-start.13
  675.6 6.7 collective-permute-start.15
  679.9 3.9 collective-permute-start.14
  683.9 5.6 collective-permute-start.16
  685.2 5.3 collective-permute-start.17
Sparse Core Ops, SparseCore 0:
  23.1 79.1 all-gather.7
